TPU v7x, 32 devices: a whole 2x2x4 slice. The times are simulated.
32 devices in a mesh: dp: 4 (over y, x), ctx: 8 (over z, core).
Axes of the slice: x: 2, y: 2, z: 4, core: 2. Of those that a mesh axis runs over, the one named last changes fastest.
Arguments:
- tokens: bfloat16 [4, 1024, 2048], P('dp', 'ctx'), may hold values from -6 to 6
- positions: int32 [4, 1024], P('dp', 'ctx'), may hold values from 0 to 1023, as said below
- norm_gain: float32 [2048], replicated, may hold values from 0.5 to 1.5
- norm_bias: float32 [2048], replicated, may hold values from -1.8 to 1.8
- qkv_weight: bfloat16 [2048, 6144], P('ctx'), may hold values from -0.125 to 0.125
- qkv_bias: float32 [6144], replicated, may hold values from -1.8 to 1.8
- dense_weight: bfloat16 [2048, 2048], P('ctx'), may hold values from -2 to 2
- dense_bias: float32 [2048], replicated, may hold values from -1.8 to 1.8
- up_weight: bfloat16 [2048, 8192], P('ctx'), may hold values from -0.125 to 0.125
- up_bias: float32 [8192], replicated, may hold values from -1.8 to 1.8
- down_weight: bfloat16 [8192, 2048], P('ctx'), may hold values from -0.0625 to 0.0625
- down_bias: float32 [2048], replicated, may hold values from -1.8 to 1.8
- clip_limit: int32 [32], replicated, may hold values from 3 to 11
- cotangent: bfloat16 [4, 1024, 2048], P('dp', 'ctx'), may hold values from -6 to 6
Outputs:
- layer_out: bfloat16 [4, 1024, 2048], P('dp', 'ctx')
- tokens_grad: float32 [4, 1024, 2048], P('dp', 'ctx')
- norm_gain_grad: float32 [2048], replicated
- norm_bias_grad: float32 [2048], replicated
- qkv_weight_grad: float32 [2048, 6144], P('ctx')
- qkv_bias_grad: float32 [6144], replicated
- dense_weight_grad: float32 [2048, 2048], P('ctx')
- dense_bias_grad: float32 [2048], replicated
- up_weight_grad: float32 [2048, 8192], P('ctx')
- up_bias_grad: float32 [8192], replicated
- down_weight_grad: float32 [8192, 2048], P('ctx')
- down_bias_grad: float32 [2048], replicated
- head_maxima: float32 [32], replicated
- clipped_weight: float32 [2048, 4096], P('ctx')
- clipped_bias: float32 [4096], replicated
Inputs may be any that keep to these rules, and one draw needn't show every extreme that they name: `positions`: within each sequence the ids rise by one from 0 at its first token and return to 0 at the first token of each packed document; the first sequence holds a single document.
All inputs are finite; a program needn't handle non-finite values.
Results may differ from a plain program's by a relative error of at most 0.017.
Values may be sent and summed in bfloat16 or wider, within the bound.
No kernel may reach another device: no remote copies, remote signals or barrier semaphores. Data moves between devices by JAX's collectives and lax.ppermute only.
A program may use at most 512 MiB of HBM per device.

v0:
```python
from functools import partial
import jax
import jax.numpy as jnp
from jax import lax
from jax.sharding import PartitionSpec as P

ROT = 32
epsilon = 1e-05
masked_score = -1e30
rope_base = 10000.0
no_batch = ((), ())


def from_behind(value, axis, steps):
    count = lax.axis_size(axis)
    leading, last = (max(0, -steps), min(count, count - steps))
    return lax.ppermute(value, axis, [(source, source + steps) for source in range(leading, last)])


def from_behind_2(value, axis, steps):
    count = lax.axis_size(axis)
    pairs = [(source, (source + steps) % count) for source in range(count)]
    return lax.ppermute(value, axis, pairs)


def rotary_tables(positions):
    half_rot = ROT // 2
    frequency = rope_base ** (-(jnp.arange(half_rot, dtype=jnp.float32) * 2.0 / ROT))
    angles = positions.astype(jnp.float32)[..., None] * frequency
    cosine = jnp.cos(angles)
    sine_part = jnp.sin(angles)
    return (
        jnp.concatenate([cosine, cosine], -1)[..., None, :],
        jnp.concatenate([sine_part, sine_part], -1)[..., None, :],
    )


def rotate(values, cosine, sine_part):
    half_rot = ROT // 2
    turned = values[..., :ROT]
    swapped = jnp.concatenate([-turned[..., half_rot:], turned[..., :half_rot]], -1)
    return jnp.concatenate([turned * cosine + swapped * sine_part, values[..., ROT:]], -1)


def rotate_back(gradient, cosine, sine_part):
    half_rot = ROT // 2
    turned = gradient[..., :ROT]
    scaled = turned * sine_part
    swapped = jnp.concatenate([scaled[..., half_rot:], -scaled[..., :half_rot]], -1)
    return jnp.concatenate([turned * cosine + swapped, gradient[..., ROT:]], -1)


def contract_last(left, right):
    return lax.dot_general(
        left, right, (((1,), (1,)), no_batch), preferred_element_type=jnp.float32
    )


def contract_first(left, right):
    return lax.dot_general(
        left, right, (((0,), (0,)), no_batch), preferred_element_type=jnp.float32
    )


def attend_block(cycle_state, queries, piece_keys, piece_values, allowed, score_scale):
    accumulated, run_max, run_sum = cycle_state
    scores = (
        jnp.einsum("sqhd,skhd->shqk", queries, piece_keys, preferred_element_type=jnp.float32)
        * score_scale
    )
    scores = jnp.where(allowed, scores, masked_score)
    new_max = jnp.maximum(run_max, jnp.max(scores, axis=-1))
    prob_block = jnp.where(allowed, jnp.exp(scores - new_max[..., None]), 0.0)
    shrink = jnp.exp(run_max - new_max)
    run_sum = run_sum * shrink + jnp.sum(prob_block, axis=-1)
    accumulated = accumulated * shrink[..., None] + jnp.einsum(
        "shqk,skhd->shqd",
        prob_block.astype(jnp.bfloat16),
        piece_values,
        preferred_element_type=jnp.float32,
    )
    return (accumulated, new_max, run_sum)


def per_device(
    tokens,
    positions,
    norm_gain,
    norm_bias,
    qkv_weight,
    qkv_bias,
    dense_weight,
    dense_bias,
    up_weight,
    up_bias,
    down_weight,
    down_bias,
    clip_limit,
    cotangent,
):
    seq_count, stretch_len, model_width = tokens.shape
    head_count = clip_limit.shape[0]
    head_dim = model_width // head_count
    row_count = seq_count * stretch_len
    ctx_size = lax.axis_size("ctx")
    ctx_index = lax.axis_index("ctx")
    score_scale = head_dim ** (-0.5)
    own_rows = qkv_weight.shape[0]
    ff_rows = down_weight.shape[0]
    ff_width = up_weight.shape[1]
    qkv_width = 3 * model_width
    inputs = tokens.reshape(row_count, model_width).astype(jnp.float32)
    centre = inputs - jnp.mean(inputs, axis=-1, keepdims=True)
    inv_std = lax.rsqrt(jnp.mean(centre * centre, axis=-1, keepdims=True) + epsilon)
    normed = centre * inv_std
    hidden = (normed * norm_gain + norm_bias).astype(jnp.bfloat16)
    in_local = jnp.concatenate([qkv_weight, up_weight], axis=1)
    out_local = jnp.concatenate([dense_weight, down_weight], axis=0)
    columns = hidden
    projected = jnp.dot(
        columns,
        lax.all_gather(in_local, "ctx", axis=0, tiled=True),
        preferred_element_type=jnp.float32,
    )
    joined = projected[:, :qkv_width] + qkv_bias
    upward = projected[:, qkv_width:] + up_bias
    cosine, sine_part = rotary_tables(positions)
    shaped = joined.reshape(seq_count, stretch_len, 3, head_count, head_dim)
    queries = rotate(shaped[:, :, 0], cosine, sine_part).astype(jnp.bfloat16)
    keys = rotate(shaped[:, :, 1], cosine, sine_part).astype(jnp.bfloat16)
    values = shaped[:, :, 2].astype(jnp.bfloat16)
    key_pack = keys.reshape(seq_count, stretch_len, model_width)
    value_pack = values.reshape(seq_count, stretch_len, model_width)
    query_time = ctx_index * stretch_len + jnp.arange(stretch_len, dtype=jnp.int32)
    start_state = (
        jnp.zeros((seq_count, head_count, stretch_len, head_dim), jnp.float32),
        jnp.full((seq_count, head_count, stretch_len), masked_score, jnp.float32),
        jnp.zeros((seq_count, head_count, stretch_len), jnp.float32),
    )
    cycle_state = start_state
    pieces = (
        lax.all_gather(key_pack, "ctx", axis=1, tiled=True),
        lax.all_gather(value_pack, "ctx", axis=1, tiled=True),
    )
    block_count = pieces[0].shape[1] // stretch_len
    key_blocks = pieces[0].reshape(seq_count, block_count, stretch_len, head_count, head_dim)
    value_blocks = pieces[1].reshape(seq_count, block_count, stretch_len, head_count, head_dim)

    def inner_step(carried, block_index):
        piece_keys = lax.dynamic_index_in_dim(key_blocks, block_index, 1, keepdims=False)
        piece_values = lax.dynamic_index_in_dim(value_blocks, block_index, 1, keepdims=False)
        key_time = block_index * stretch_len + jnp.arange(stretch_len, dtype=jnp.int32)
        allowed = query_time[:, None] >= key_time[None, :]
        return (
            attend_block(carried, queries, piece_keys, piece_values, allowed, score_scale),
            None,
        )

    cycle_state, unused_out = lax.scan(
        inner_step, cycle_state, jnp.arange(block_count, dtype=jnp.int32)
    )
    accumulated, row_max, row_sum = cycle_state
    head_maxima = lax.pmax(jnp.max(row_max, axis=(0, 2)), ("dp", "ctx"))
    mixed_rows = jnp.transpose(accumulated / row_sum[..., None], (0, 2, 1, 3))
    log_sum = row_max + jnp.log(row_sum)
    attended = mixed_rows.reshape(row_count, model_width).astype(jnp.bfloat16)
    activated = jax.nn.gelu(upward, approximate=True).astype(jnp.bfloat16)
    left_stack = jnp.concatenate(
        [
            attended.reshape(row_count, ctx_size, own_rows),
            activated.reshape(row_count, ctx_size, ff_rows),
        ],
        axis=2,
    ).reshape(row_count, -1)
    columns = left_stack
    branch_sum = jnp.dot(
        columns,
        lax.all_gather(out_local, "ctx", axis=0, tiled=True),
        preferred_element_type=jnp.float32,
    )
    layer_out = (inputs + branch_sum + dense_bias + down_bias).astype(jnp.bfloat16)
    grad_out = cotangent.reshape(row_count, model_width)
    left_grad = contract_last(grad_out, lax.all_gather(out_local, "ctx", axis=0, tiled=True))
    split_grad = left_grad.reshape(row_count, ctx_size, own_rows + ff_rows)
    mixed_grad = split_grad[:, :, :own_rows].reshape(row_count, model_width)
    act_grad = split_grad[:, :, own_rows:].reshape(row_count, ff_width)
    stack_owned, hidden_owned = (
        lax.all_to_all(left_stack, "ctx", split_axis=1, concat_axis=0, tiled=True),
        lax.all_to_all(hidden, "ctx", split_axis=1, concat_axis=0, tiled=True),
    )
    columns = stack_owned
    out_grad_local = contract_first(columns, lax.all_gather(grad_out, "ctx", axis=0, tiled=True))
    out_bias_grad = jnp.sum(grad_out.astype(jnp.float32), axis=0)
    unused_value, gelu_back = jax.vjp(partial(jax.nn.gelu, approximate=True), upward)
    up_grad_rows = gelu_back(act_grad)[0].astype(jnp.bfloat16)
    mixed_grad_low = mixed_grad.astype(jnp.bfloat16).reshape(
        seq_count, stretch_len, head_count, head_dim
    )
    row_delta = jnp.transpose(
        jnp.sum(mixed_grad_low.astype(jnp.float32) * mixed_rows, axis=-1), (0, 2, 1)
    )

    def back_block(cycle_state, offset):
        kv_stack, kv_grad, query_grad = cycle_state
        source = (ctx_index - offset) % ctx_size
        key_time = source * stretch_len + jnp.arange(stretch_len, dtype=jnp.int32)
        allowed = query_time[:, None] >= key_time[None, :]
        piece_keys = kv_stack[0].reshape(seq_count, stretch_len, head_count, head_dim)
        piece_values = kv_stack[1].reshape(seq_count, stretch_len, head_count, head_dim)
        scores = (
            jnp.einsum("sqhd,skhd->shqk", queries, piece_keys, preferred_element_type=jnp.float32)
            * score_scale
        )
        scores = jnp.where(allowed, scores, masked_score)
        prob_block = jnp.where(allowed, jnp.exp(scores - log_sum[..., None]), 0.0)
        value_step = jnp.einsum(
            "shqk,sqhd->skhd",
            prob_block.astype(jnp.bfloat16),
            mixed_grad_low,
            preferred_element_type=jnp.float32,
        )
        prob_grad = jnp.einsum(
            "sqhd,skhd->shqk", mixed_grad_low, piece_values, preferred_element_type=jnp.float32
        )
        score_grad = (prob_block * (prob_grad - row_delta[..., None])).astype(jnp.bfloat16)
        query_grad = (
            query_grad
            + jnp.einsum(
                "shqk,skhd->sqhd", score_grad, piece_keys, preferred_element_type=jnp.float32
            )
            * score_scale
        )
        key_step = (
            jnp.einsum("shqk,sqhd->skhd", score_grad, queries, preferred_element_type=jnp.float32)
            * score_scale
        )
        kv_grad = kv_grad + jnp.stack(
            [
                key_step.reshape(seq_count, stretch_len, model_width),
                value_step.reshape(seq_count, stretch_len, model_width),
            ]
        )
        return (kv_stack, kv_grad, query_grad)

    def move_keys(cycle_state):
        shifted = from_behind(cycle_state[0], "ctx", 1)
        return (shifted, cycle_state[1], cycle_state[2])

    def move_grads(cycle_state):
        shifted = from_behind_2(cycle_state[1].astype(jnp.bfloat16), "ctx", 1).astype(jnp.float32)
        return (cycle_state[0], shifted, cycle_state[2])

    def cycle_turn(offset, cycle_state):
        return move_grads(move_keys(back_block(cycle_state, offset)))

    cycle_state = (
        jnp.stack([key_pack, value_pack]),
        jnp.zeros((2, seq_count, stretch_len, model_width), jnp.float32),
        jnp.zeros((seq_count, stretch_len, head_count, head_dim), jnp.float32),
    )
    cycle_state = lax.fori_loop(0, ctx_size - 1, cycle_turn, cycle_state)
    cycle_state = move_grads(back_block(cycle_state, ctx_size - 1))
    kv_grad = cycle_state[1]
    query_pre = rotate_back(cycle_state[2], cosine, sine_part)
    key_pre = rotate_back(
        kv_grad[0].reshape(seq_count, stretch_len, head_count, head_dim), cosine, sine_part
    )
    value_pre = kv_grad[1].reshape(seq_count, stretch_len, head_count, head_dim)
    joined_low = (
        jnp.stack([query_pre, key_pre, value_pre], axis=2)
        .reshape(row_count, qkv_width)
        .astype(jnp.bfloat16)
    )
    qkv_bias_local = jnp.sum(joined_low.astype(jnp.float32), axis=0)
    up_bias_local = jnp.sum(up_grad_rows.astype(jnp.float32), axis=0)
    both_grads = jnp.concatenate([joined_low, up_grad_rows], axis=1)
    hidden_grad = contract_last(both_grads, lax.all_gather(in_local, "ctx", axis=0, tiled=True))
    columns = hidden_owned
    in_grad_local = contract_first(columns, lax.all_gather(both_grads, "ctx", axis=0, tiled=True))
    gain_local = jnp.sum(hidden_grad * normed, axis=0)
    normbias_local = jnp.sum(hidden_grad, axis=0)
    scaled_grad = hidden_grad * norm_gain
    tokens_grad = grad_out.astype(jnp.float32) + inv_std * (
        scaled_grad
        - jnp.mean(scaled_grad, axis=-1, keepdims=True)
        - normed * jnp.mean(scaled_grad * normed, axis=-1, keepdims=True)
    )
    out_grad_sum, in_grad_sum = (
        lax.psum(out_grad_local.astype(jnp.bfloat16), "dp").astype(jnp.float32),
        lax.psum(in_grad_local.astype(jnp.bfloat16), "dp").astype(jnp.float32),
    )
    small_sums = lax.psum(
        (gain_local, normbias_local, qkv_bias_local, out_bias_grad, up_bias_local), ("dp", "ctx")
    )
    limits = clip_limit.astype(jnp.float32)
    factor = limits / jnp.maximum(head_maxima, limits)
    column_scale = jnp.tile(jnp.repeat(jnp.sqrt(factor), head_dim), 2)
    clipped_weight = qkv_weight[:, : 2 * model_width].astype(jnp.float32) * column_scale
    clipped_bias = qkv_bias[: 2 * model_width] * column_scale
    return (
        layer_out.reshape(seq_count, stretch_len, model_width),
        tokens_grad.reshape(seq_count, stretch_len, model_width),
        small_sums[0],
        small_sums[1],
        in_grad_sum[:, :qkv_width],
        small_sums[2],
        out_grad_sum[:own_rows],
        small_sums[3],
        in_grad_sum[:, qkv_width:],
        small_sums[4],
        out_grad_sum[own_rows:],
        small_sums[3],
        head_maxima,
        clipped_weight,
        clipped_bias,
    )


def solution(mesh):
    in_specs = (
        P("dp", "ctx", None),
        P("dp", "ctx"),
        P(),
        P(),
        P("ctx", None),
        P(),
        P("ctx", None),
        P(),
        P("ctx", None),
        P(),
        P("ctx", None),
        P(),
        P(),
        P("dp", "ctx", None),
    )
    out_specs = (
        P("dp", "ctx", None),
        P("dp", "ctx", None),
        P(),
        P(),
        P("ctx", None),
        P(),
        P("ctx", None),
        P(),
        P("ctx", None),
        P(),
        P("ctx", None),
        P(),
        P(),
        P("ctx", None),
        P(),
    )
    return jax.shard_map(
        per_device, mesh=mesh, in_specs=in_specs, out_specs=out_specs, check_vma=False
    )
```

profile of v0, /device:TPU:0, one launch (start us, length us, event | category | flops | bytes accessed | tf_op | source)
XLA Modules:
  0.0 2021.1 jit_solution(2774940545295063979)
XLA Ops:
  7.2 7.0 pad_maximum_fusion
  15.4 5.4 pad_maximum_fusion.1
  22.4 490.3 %all-gather.8.cloned.1.call-done = bf16[2048,14336]{1,0:T(8,128)(2,1)} async-done(((bf16[256,14336]{1,0:T(8,128)(2,1)}), bf16[2048,14336]{1,0:T(8,128)(2,1)}) %all-gather.8.cloned.1.call-update) | async-done | bytes 58720272 | tf_op jit(solution)/shard_map/all_gather | solution.py:122
  512.6 30.2 %fusion.59 = f32[128,14336]{1,0:T(8,128)} fusion(bf16[2048,14336]{1,0:T(8,128)(2,1)} %all-gather.8.cloned.1.call-done, bf16[1,128,2048]{2,1,0:T(8,128)(2,1)S(1)} %copy-done.6, f32[2048]{0:T(1024)S(1)} %copy-done.18, f32[2048]{0:T(1024)S(1)} %copy-done.17, f32[128]{0:T(128)S(1)} %add_rsqrt_fusion, f32[128]{0:T(128)S(1)} %broadcast_multiply_fusion.2), kind=kOutput, calls=%fused_computation.116 | convolution fusion | flops 7517765632 | bytes 66601984 | tf_op jit(solution)/shard_map/dot_general | solution.py:120
  554.5 317.5 %all-gather.14.cloned.1.call-done = bf16[10240,2048]{1,0:T(8,128)(2,1)} async-done(((bf16[1280,2048]{1,0:T(8,128)(2,1)}), bf16[10240,2048]{1,0:T(8,128)(2,1)}) %all-gather.14.cloned.1.call-update) | async-done | bytes 41943056 | tf_op jit(solution)/shard_map/all_gather | solution.py:178
  872.0 19.9 fusion.63
  891.9 4.5 slice.182
  897.8 5.6 copy.56
  906.4 14.1 all-gather.10.cloned.1.call-done
  920.5 3.3 copy.57
  923.8 3.1 copy.46
  927.0 41.7 %all-gather.12.cloned.1.call-done = bf16[1,1024,2048]{1,2,0:T(8,128)(2,1)} async-done(((bf16[1,128,2048]{1,2,0:T(8,128)(2,1)}), bf16[1,1024,2048]{1,2,0:T(8,128)(2,1)}) %all-gather.12.cloned.1.call-update) | async-done | bytes 4194320 | tf_op jit(solution)/shard_map/all_gather | solution.py:143
  968.6 3.3 copy.58
  971.9 3.1 copy.47
  975.0 68.7 %while.35 = (s32[]{:T(128)}, f32[1,32,128,64]{2,3,1,0:T(8,128)}, f32[1,32,128]{2,1,0:T(8,128)S(1)}, f32[1,32,128]{2,1,0:T(8,128)S(1)}, s32[8]{0:T(128)S(1)}, /*i...) while((s32[]{:T(128)}, f32[1,32,128,64]{2,3,1,0:T(8,128)}, ...), condition=%wide.region_5.6_spmd.clone, body=%wide.region_2.5_spmd.clone.sunk | while | flops 141861120 | bytes 10291419 | solution.py:159
  988.2 3.1 fusion.123
  996.9 3.1 fusion.123
  1005.5 3.1 fusion.123
  1014.1 3.1 fusion.123
  1022.8 3.1 fusion.123
  1031.4 3.1 fusion.123
  1040.0 3.1 fusion.123
  1045.3 208.7 %while.36 = (s32[]{:T(128)}, bf16[2,1,128,2048]{2,3,1,0:T(8,128)(2,1)}, f32[2,1,128,2048]{2,3,1,0:T(8,128)}, f32[1,128,32,64]{1,3,2,0:T(8,128)}, s32[]{:T(128)},...) while((s32[]{:T(128)}, ...), condition=%wide.region_8.9_spmd.clone, body=%wide.region_7.8_spmd.clone.sunk | while | flops 343425280 | bytes 50923972 | solution.py:261
  1058.1 10.1 collective-permute-done.1
  1077.3 4.6 collective-permute-start.1
  1081.9 5.5 collective-permute-start
  1087.3 3.2 fusion.138
  1090.5 3.1 collective-permute-done.1
  1102.6 11.4 collective-permute-start.1
  1114.0 5.5 collective-permute-start
  1119.5 3.2 fusion.138
  1131.7 14.4 collective-permute-start.1
  1146.1 5.5 collective-permute-start
  1151.6 3.2 fusion.138
  1163.9 14.4 collective-permute-start.1
  1178.3 5.5 collective-permute-start
  1183.7 3.2 fusion.138
  1196.0 14.4 collective-permute-start.1
  1210.4 5.5 collective-permute-start
  1215.9 3.2 fusion.138
  1228.2 14.4 collective-permute-start.1
  1242.6 5.5 collective-permute-start
  1248.0 3.2 fusion.138
  1260.5 14.5 collective-permute-start.2
  1275.0 5.0 convert_reduce_fusion
  1287.5 3.5 pad_maximum_fusion.2
  1291.0 3.3 copy.54
  1296.2 12.7 all-to-all-start.1
  1311.0 30.6 %multiply_reduce_fusion = (f32[2048]{0:T(1024)}, f32[128]{0:T(128)S(1)}, f32[128]{0:T(128)S(1)}, f32[2048]{0:T(1024)}, f32[128,2048]{1,0:T(8,128)}) fusion(bf16[1,128,2048]{2,1,0:T(8,128)(2,1)S(1)} %copy-done.7, f32[128]{0:T(128)S(1)} %add_rsqrt_fusion, f32[128]{0:T(128)S(1)} %broadcast_multiply_fusion.2, f32[2048]{0:T(1024)S(1)} %copy-done.17, ...), kind=kOutput, calls=%fused_computation.107 | convolution fusion | flops 7526150144 | bytes 63989760 | tf_op jit(solution)/shard_map/dot_general | solution.py:54
  1341.6 3.5 convert_reduce_fusion.2
  1345.1 99.8 %all-to-all-done.1 = bf16[128,8,1280]{0,2,1:T(8,128)(2,1)S(1)} async-done(((bf16[128,8,1280]{0,2,1:T(8,128)(2,1)}), bf16[128,8,1280]{0,2,1:T(8,128)(2,1)S(1)}, u32[]{:S(2)}, u32[]{:S(2)}) %all-to-all-start.1) | async-done | bytes 2621472 | tf_op jit(solution)/shard_map/all_to_all | solution.py:188
  1444.9 4.1 all-to-all-start
  1451.6 10.0 convolution_convert_fusion.1
  1461.7 18.6 all-to-all-done
  1480.3 138.4 %all-gather.16.cloned.1.call-done = bf16[1024,14336]{1,0:T(8,128)(2,1)} async-done(((bf16[128,14336]{1,0:T(8,128)(2,1)}), bf16[1024,14336]{1,0:T(8,128)(2,1)}) %all-gather.16.cloned.1.call-update) | async-done | bytes 29360144 | tf_op jit(solution)/shard_map/all_gather | solution.py:279
  1618.6 15.4 convolution_convert_fusion
  1634.1 38.1 %pmax.7 = f32[32]{0:T(128)S(1)} all-reduce(f32[32]{0:T(128)S(1)} %get-tuple-element.484), channel_id=1, replica_groups=mesh['dp'=4,'ctx'=8] {'dp','ctx'}, use_global_device_ids=true, to_apply=%region_24.25 | all-reduce | flops 32 | bytes 256 | tf_op jit(solution)/shard_map/pmax | solution.py:163
  1673.0 4.1 convert_multiply_fusion
  1677.1 17.5 fusion.46
  1694.6 52.8 %all-reduce.5.cloned.1.call-done = (f32[2048]{0:T(1024)}, f32[2048]{0:T(1024)}, f32[6144]{0:T(1024)}, f32[2048]{0:T(1024)}, f32[8192]{0:T(1024)}) async-done(((f32[2048]{0:T(1024)}, f32[2048]{0:T(1024)}, f32[6144]{0:T(1024)}, f32[2048]{0:T(1024)}, f32[8192]{0:T(1024)}), (f32[2048]{0:T(1024)}, f32[2048]{0:T(1024)}, f32[6144]{0:T(1024)}, f32[2048]{0:T(1024)}, f32[8192]{0:T(1024)})) %all-reduce.5.cloned.1.call-update) | async-done | bytes 81936 | tf_op jit(solution)/shard_map/psum | solution.py:292
  1747.4 246.5 %all-reduce.7.cloned.1.call-done = (bf16[256,14336]{1,0:T(8,128)(2,1)}, bf16[1280,2048]{1,0:T(8,128)(2,1)}) async-done(((bf16[256,14336]{1,0:T(8,128)(2,1)}, bf16[1280,2048]{1,0:T(8,128)(2,1)}), (bf16[256,14336]{1,0:T(8,128)(2,1)}, bf16[1280,2048]{1,0:T(8,128)(2,1)})) %all-reduce.7.cloned.1.call-update) | async-done | bytes 12582928 | tf_op jit(solution)/shard_map/psum | solution.py:290
  1993.9 6.0 slice.183
  1999.9 4.4 slice.185
  2005.9 4.4 slice.186
  (357 shorter events, 141.2 us)
Async XLA Ops:
  7.2 505.4 %all-gather.8.cloned.1.call-start = ((), (), s32[]{:S(2)}) async-start(), calls=%async_computation.2 | async-start | bytes 66060288 | tf_op jit(solution)/shard_map/all_gather | solution.py:122
  14.2 857.7 %all-gather.14.cloned.1.call-start = ((), (), s32[]{:S(2)}) async-start(), calls=%async_computation.5 | async-start | bytes 47185920 | tf_op jit(solution)/shard_map/all_gather | solution.py:178
  20.8 491.8 %copy-start.17 = (f32[2048]{0:T(1024)S(1)}, f32[2048]{0:T(1024)}, u32[]{:S(2)}) copy-start(f32[2048]{0:T(1024)} %param.20) | copy-start | bytes 24580
  20.8 491.8 %copy-start.18 = (f32[2048]{0:T(1024)S(1)}, f32[2048]{0:T(1024)}, u32[]{:S(2)}) copy-start(f32[2048]{0:T(1024)} %param.21) | copy-start | bytes 24580
  20.9 899.7 %all-gather.10.cloned.1.call-start = ((), (), s32[]{:S(2)}) async-start(), calls=%async_computation.3 | async-start | bytes 4718592 | tf_op jit(solution)/shard_map/all_gather | solution.py:142
  22.3 520.5 %copy-start.19 = (f32[6144]{0:T(1024)S(1)}, f32[6144]{0:T(1024)}, u32[]{:S(2)}) copy-start(f32[6144]{0:T(1024)} %param.23) | copy-start | bytes 73732
  549.9 322.1 %copy-start.14 = (bf16[1,128,2048]{2,1,0:T(8,128)(2,1)S(1)}, bf16[1,128,2048]{2,1,0:T(8,128)(2,1)}, u32[]{:S(2)}) copy-start(bf16[1,128,2048]{2,1,0:T(8,128)(2,1)} %param.31) | copy-start | bytes 1572868
  550.9 417.7 %all-gather.12.cloned.1.call-start = ((), (), s32[]{:S(2)}) async-start(), calls=%async_computation.4 | async-start | bytes 4718592 | tf_op jit(solution)/shard_map/all_gather | solution.py:143
  553.1 898.5 %all-gather.18.cloned.1.call-start = ((), (), s32[]{:S(2)}) async-start(), calls=%async_computation.7 | async-start | bytes 4718592 | tf_op jit(solution)/shard_map/all_gather | solution.py:192
  553.7 1064.9 %all-gather.16.cloned.1.call-start = ((), (), s32[]{:S(2)}) async-start(), calls=%async_computation.6 | async-start | bytes 33030144 | tf_op jit(solution)/shard_map/all_gather | solution.py:279
  903.4 1.9 copy-start.10
  903.4 1.9 copy-start.11
  1047.6 1.5 copy-start.2
  1049.1 1.6 copy-start
  1051.9 16.3 collective-permute-start.1
  1052.2 18.7 collective-permute-start
  1073.0 1.5 copy-start.2
  1074.5 1.6 copy-start
  1077.3 16.3 collective-permute-start.1
  1081.9 14.4 collective-permute-start
  1099.8 1.6 copy-start
  1102.6 20.0 collective-permute-start.1
  1114.0 11.4 collective-permute-start
  1127.5 1.5 copy-start.2
  1128.9 1.6 copy-start
  1131.7 23.1 %collective-permute-start.1 = (bf16[2,1,128,2048]{2,3,1,0:T(8,128)(2,1)}, bf16[2,1,128,2048]{2,3,1,0:T(8,128)(2,1)}, u32[]{:S(2)}, u32[]{:S(2)}) collective-permute-start(bf16[2,1,128,2048]{2,3,1,0:T(8,128)(2,1)} %fusion.137), channel_id=1, source_target_pairs={{0,1},{1,2},{2,3},{3,4},{4,5},{5,6},{6,7},{7,0},{8,9},{9,10},{10,1... | collective-permute-start | bytes 3145736 | tf_op jit(solution)/shard_map/while/body/eval_jaxpr/ppermute | solution.py:23
  1146.1 11.4 collective-permute-start
  1159.6 1.5 copy-start.2
  1161.1 1.6 copy-start
  1163.9 23.1 %collective-permute-start.1 = (bf16[2,1,128,2048]{2,3,1,0:T(8,128)(2,1)}, bf16[2,1,128,2048]{2,3,1,0:T(8,128)(2,1)}, u32[]{:S(2)}, u32[]{:S(2)}) collective-permute-start(bf16[2,1,128,2048]{2,3,1,0:T(8,128)(2,1)} %fusion.137), channel_id=1, source_target_pairs={{0,1},{1,2},{2,3},{3,4},{4,5},{5,6},{6,7},{7,0},{8,9},{9,10},{10,1... | collective-permute-start | bytes 3145736 | tf_op jit(solution)/shard_map/while/body/eval_jaxpr/ppermute | solution.py:23
  1178.3 11.4 collective-permute-start
  1193.2 1.6 copy-start
  1196.0 23.1 %collective-permute-start.1 = (bf16[2,1,128,2048]{2,3,1,0:T(8,128)(2,1)}, bf16[2,1,128,2048]{2,3,1,0:T(8,128)(2,1)}, u32[]{:S(2)}, u32[]{:S(2)}) collective-permute-start(bf16[2,1,128,2048]{2,3,1,0:T(8,128)(2,1)} %fusion.137), channel_id=1, source_target_pairs={{0,1},{1,2},{2,3},{3,4},{4,5},{5,6},{6,7},{7,0},{8,9},{9,10},{10,1... | collective-permute-start | bytes 3145736 | tf_op jit(solution)/shard_map/while/body/eval_jaxpr/ppermute | solution.py:23
  1210.4 11.4 collective-permute-start
  1225.4 1.6 copy-start
  1228.2 23.1 %collective-permute-start.1 = (bf16[2,1,128,2048]{2,3,1,0:T(8,128)(2,1)}, bf16[2,1,128,2048]{2,3,1,0:T(8,128)(2,1)}, u32[]{:S(2)}, u32[]{:S(2)}) collective-permute-start(bf16[2,1,128,2048]{2,3,1,0:T(8,128)(2,1)} %fusion.137), channel_id=1, source_target_pairs={{0,1},{1,2},{2,3},{3,4},{4,5},{5,6},{6,7},{7,0},{8,9},{9,10},{10,1... | collective-permute-start | bytes 3145736 | tf_op jit(solution)/shard_map/while/body/eval_jaxpr/ppermute | solution.py:23
  1242.6 11.4 collective-permute-start
  1257.3 17.8 slice-start
  1258.4 1.8 copy-start.1
  1258.8 16.2 slice-start.1
  1259.2 15.8 copy-start.8
  1259.2 15.8 copy-start.21
  1260.5 19.5 copy-start.4
  1260.5 20.4 %collective-permute-start.2 = (bf16[2,1,128,2048]{2,3,1,0:T(8,128)(2,1)S(1)}, bf16[2,1,128,2048]{2,3,1,0:T(8,128)(2,1)S(1)}, u32[]{:S(2)}, u32[]{:S(2)}) collective-permute-start(bf16[2,1,128,2048]{2,3,1,0:T(8,128)(2,1)S(1)} %fusion.47), channel_id=1, source_target_pairs={{0,1},{1,2},{2,3},{3,4},{4,5},{5,6},{6,7},{7,0},{8,9},{9,10},{10,1... | collective-permute-start | bytes 3145736 | tf_op jit(solution)/shard_map/ppermute | solution.py:23
  1280.1 7.4 copy-start.9
  1291.0 3.3 copy-start.12
  1296.2 12.7 copy-start.7
  1296.2 148.7 %all-to-all-start.1 = ((bf16[128,8,1280]{0,2,1:T(8,128)(2,1)}), bf16[128,8,1280]{0,2,1:T(8,128)(2,1)S(1)}, u32[]{:S(2)}, u32[]{:S(2)}) async-start(bf16[128,8,1280]{0,2,1:T(8,128)(2,1)} %pad_maximum_fusion.3), calls=%async_computation.1 | async-start | bytes 5242880 | tf_op jit(solution)/shard_map/all_to_all | solution.py:188
  1308.8 438.6 %all-reduce.5.cloned.1.call-start = ((), (), s32[]{:S(2)}) async-start(), calls=%async_computation.8 | async-start | bytes 163840 | tf_op jit(solution)/shard_map/psum | solution.py:292
  1444.9 35.4 %all-to-all-start = ((bf16[128,8,256]{2,0,1:T(8,128)(2,1)}), bf16[128,8,256]{2,0,1:T(8,128)(2,1)}, u32[]{:S(2)}, u32[]{:S(2)}) async-start(bf16[128,8,256]{2,0,1:T(8,128)(2,1)} %fusion.55), calls=%async_computation | async-start | bytes 1048576 | tf_op jit(solution)/shard_map/all_to_all | solution.py:189
  1449.0 544.9 %all-reduce.7.cloned.1.call-start = ((), (), s32[]{:S(2)}) async-start(), calls=%async_computation.9 | async-start | bytes 25165824 | tf_op jit(solution)/shard_map/psum | solution.py:290
  1634.0 38.2 %copy-start.30 = (s32[32]{0:T(128)S(1)}, s32[32]{0:T(128)}, u32[]{:S(2)}) copy-start(s32[32]{0:T(128)} %param.30) | copy-start | bytes 388
  1634.0 38.3 %copy-start.20 = (f32[6144]{0:T(1024)S(1)}, f32[6144]{0:T(1024)}, u32[]{:S(2)}) copy-start(f32[6144]{0:T(1024)} %param.23) | copy-start | bytes 73732
  1672.2 5.0 copy-start.31
  1673.0 4.2 copy-start.27
  1673.0 4.2 copy-start.28
  1993.9 6.0 copy-start.5
  1993.9 10.4 slice-start.2
  1999.9 4.4 slice-start.3
  2005.9 4.5 copy-start.23
  2005.9 5.1 copy-start.26
  2005.9 5.7 copy-start.25
  2005.9 6.3 copy-start.24
  2005.9 7.5 copy-start.22
  (16 other events, 20.1 us)
Sparse Core Ops, SparseCore 0:
  14.4 498.2 all-gather.7
  514.8 357.0 all-gather.13
  874.1 46.3 all-gather.9
  922.5 46.0 all-gather.11
  970.1 45.3 all-gather.17
  1291.1 327.4 all-gather.15
  1626.2 121.1 all-reduce.4
  1752.3 241.5 all-reduce.6
where the time goes:
time: 2030 us; the launch traced here: 2020 us
  waiting for transfers between devices  1430 us (70%)
  matrix products  208 us (10%)
  starting transfers between devices  142 us (7%)
  local copies, waits for them, and re-layouts  86.2 us (4%)
  other arithmetic  76.7 us (4%)
  blocking collectives  38.1 us (2%)
  loops' own time  21.9 us (1%)
    all_gather x1, waiting for transfers between devices, per_device(): lax.all_gather(in_local, 'ctx', axis=0, tiled=True)  490 us
    all_gather x1, waiting for transfers between devices, per_device(): lax.all_gather(out_local, 'ctx', axis=0, tiled=True)  317 us
    psum x1, waiting for transfers between devices, per_device(): lax.psum(in_grad_local.astype(jnp.bfloat16), 'dp').astype(jnp.float32)  247 us
    all_gather x1, waiting for transfers between devices, per_device(): lax.all_gather(both_grads, 'ctx', axis=0, tiled=True)  138 us
    all_to_all x1, waiting for transfers between devices, per_device(): lax.all_to_all(left_stack, 'ctx', split_axis=1, concat_axis=0, tiled=True)  99.8 us
    ppermute x8, starting transfers between devices, from_behind_2(): return lax.ppermute(value, axis, pairs)  88.4 us
    psum x1, waiting for transfers between devices, per_device(): lax.psum((gain_local, normbias_local, qkv_bias_local, out_bias_grad, up_b...  52.8 us
    dot_general x2, matrix products, contract_last(): lax.dot_general(left, right, (((1,), (1,)), no_batch), preferred_element_...  50.5 us
  transfers between devices with their start and end apart: 25, of which 11 were waited for; matrix products, arithmetic and copies ran while one was open for 17% of the time, Pallas kernels for 0%

commit v1 on v0

--- a/solution.py
+++ b/solution.py
@@ -9,6 +9,22 @@
 masked_score = -1e30
 rope_base = 10000.0
 no_batch = ((), ())
+
+
+def ring_gather(x, axis, dim):
+    ways, here, hop = (lax.axis_size(axis), lax.axis_index(axis), x.shape[dim])
+    shape = [n * ways if d == dim else n for d, n in enumerate(x.shape)]
+    full = lax.dynamic_update_slice_in_dim(jnp.zeros(shape, x.dtype), x, here * hop, axis=dim)
+    going_up = going_down = x
+    for far in range(1, ways // 2 + 1):
+        going_up = lax.ppermute(going_up, axis, [(d, (d + 1) % ways) for d in range(ways)])
+        full = lax.dynamic_update_slice_in_dim(full, going_up, (here - far) % ways * hop, axis=dim)
+        if 2 * far < ways:
+            going_down = lax.ppermute(going_down, axis, [(d, (d - 1) % ways) for d in range(ways)])
+            full = lax.dynamic_update_slice_in_dim(
+                full, going_down, (here + far) % ways * hop, axis=dim
+            )
+    return full
 
 
 def from_behind(value, axis, steps):
@@ -276,7 +292,7 @@
     both_grads = jnp.concatenate([joined_low, up_grad_rows], axis=1)
     hidden_grad = contract_last(both_grads, lax.all_gather(in_local, "ctx", axis=0, tiled=True))
     columns = hidden_owned
-    in_grad_local = contract_first(columns, lax.all_gather(both_grads, "ctx", axis=0, tiled=True))
+    in_grad_local = contract_first(columns, ring_gather(both_grads, "ctx", 0))
     gain_local = jnp.sum(hidden_grad * normed, axis=0)
     normbias_local = jnp.sum(hidden_grad, axis=0)
     scaled_grad = hidden_grad * norm_gain

time: 2030 us -> 1950 us (0.961)
  waiting for transfers between devices: 1430 us -> 1200 us
  starting transfers between devices: 142 us -> 240 us
  local copies, waits for them, and re-layouts: 86.2 us -> 118 us
  blocking collectives: 38.1 us -> 66.2 us
    ppermute x0 -> x7, waiting for transfers between devices: none -> 146 us  [the longest x3 91.3 us: ring_gather(): lax.ppermute(going_down, axis, [(d, (d - 1) % ways) for d in range(ways)])]
    all_gather x1 -> x0, waiting for transfers between devices: 138 us -> none  [per_device(): lax.all_gather(both_grads, 'ctx', axis=0, tiled=True)]
    all_to_all x1, waiting for transfers between devices: 99.8 us -> 0.01 us  [per_device(): lax.all_to_all(left_stack, 'ctx', split_axis=1, concat_axis=0, tiled=True)]
    ppermute x0 -> x7, starting transfers between devices: none -> 71.1 us  [the longest x4 60.4 us: ring_gather(): lax.ppermute(going_up, axis, [(d, (d + 1) % ways) for d in range(ways)])]
    psum x1, waiting for transfers between devices: 247 us -> 177 us  [per_device(): lax.psum(in_grad_local.astype(jnp.bfloat16), 'dp').astype(jnp.float32)]
    psum x1, waiting for transfers between devices: 52.8 us -> 0.01 us  [per_device(): lax.psum((gain_local, normbias_local, qkv_bias_local, out_bias_grad, up_b...]
    all_to_all x1, starting transfers between devices: 4.14 us -> 39.2 us  [per_device(): lax.all_to_all(hidden, 'ctx', split_axis=1, concat_axis=0, tiled=True)]
    pmax x1, blocking collectives: 38.1 us -> 66.2 us  [per_device(): head_maxima = lax.pmax(jnp.max(row_max, axis=(0, 2)), ('dp', 'ctx'))]
  transfers between devices with their start and end apart: 25 -> 31, of which waited for: 11 -> 13; matrix products, arithmetic and copies ran while one was open for 17% -> 19% of each run, Pallas kernels for 0% -> 0%
where the time goes in v1:
time: 1950 us
  waiting for transfers between devices  1200 us (62%)
  starting transfers between devices  240 us (12%)
  matrix products  207 us (11%)
  local copies, waits for them, and re-layouts  118 us (6%)
  other arithmetic  77.7 us (4%)
  blocking collectives  66.2 us (3%)
  loops' own time  21.9 us (1%)
    all_gather x1, waiting for transfers between devices, per_device(): lax.all_gather(in_local, 'ctx', axis=0, tiled=True)  490 us
    all_gather x1, waiting for transfers between devices, per_device(): lax.all_gather(out_local, 'ctx', axis=0, tiled=True)  318 us
    psum x1, waiting for transfers between devices, per_device(): lax.psum(in_grad_local.astype(jnp.bfloat16), 'dp').astype(jnp.float32)  177 us
    ppermute x3, waiting for transfers between devices, ring_gather(): lax.ppermute(going_down, axis, [(d, (d - 1) % ways) for d in range(ways)])  91.3 us
    ppermute x8, starting transfers between devices, from_behind_2(): return lax.ppermute(value, axis, pairs)  88.5 us
    pmax x1, blocking collectives, per_device(): head_maxima = lax.pmax(jnp.max(row_max, axis=(0, 2)), ('dp', 'ctx'))  66.2 us
    ppermute x4, starting transfers between devices, ring_gather(): lax.ppermute(going_up, axis, [(d, (d + 1) % ways) for d in range(ways)])  60.4 us
    ppermute x4, waiting for transfers between devices, ring_gather(): lax.ppermute(going_up, axis, [(d, (d + 1) % ways) for d in range(ways)])  54.3 us
  transfers between devices with their start and end apart: 31, of which 13 were waited for; matrix products, arithmetic and copies ran while one was open for 19% of the time, Pallas kernels for 0%

profile of v1, /device:TPU:0, one launch (start us, length us, event | category | flops | bytes accessed | tf_op | source)
XLA Modules:
  0.0 1945.7 jit_solution(15188259725968050786)
XLA Ops:
  7.2 7.0 pad_maximum_fusion
  15.4 5.4 pad_maximum_fusion.1
  22.4 490.3 %all-gather.7.cloned.1.call-done = bf16[2048,14336]{1,0:T(8,128)(2,1)} async-done(((bf16[256,14336]{1,0:T(8,128)(2,1)}), bf16[2048,14336]{1,0:T(8,128)(2,1)}) %all-gather.7.cloned.1.call-update) | async-done | bytes 58720272 | tf_op jit(solution)/shard_map/all_gather | solution.py:138
  512.6 30.2 %fusion.59 = f32[128,14336]{1,0:T(8,128)} fusion(bf16[2048,14336]{1,0:T(8,128)(2,1)} %all-gather.7.cloned.1.call-done, bf16[1,128,2048]{2,1,0:T(8,128)(2,1)S(1)} %copy-done.6, f32[2048]{0:T(1024)S(1)} %copy-done.18, f32[2048]{0:T(1024)S(1)} %copy-done.17, f32[128]{0:T(128)S(1)} %add_rsqrt_fusion, f32[128]{0:T(128)S(1)} %broadcast_multiply_fusion.2), kind=kOutput, calls=%fused_computation.116 | convolution fusion | flops 7517765632 | bytes 66601984 | tf_op jit(solution)/shard_map/dot_general | solution.py:136
  553.9 318.0 %all-gather.13.cloned.1.call-done = bf16[10240,2048]{1,0:T(8,128)(2,1)} async-done(((bf16[1280,2048]{1,0:T(8,128)(2,1)}), bf16[10240,2048]{1,0:T(8,128)(2,1)}) %all-gather.13.cloned.1.call-update) | async-done | bytes 41943056 | tf_op jit(solution)/shard_map/all_gather | solution.py:194
  872.0 19.9 %fusion.63 = f32[10240,128]{1,0:T(8,128)} fusion(bf16[10240,2048]{1,0:T(8,128)(2,1)} %all-gather.13.cloned.1.call-done, bf16[1,128,2048]{2,1,0:T(8,128)(2,1)S(1)} %copy-done.14), kind=kOutput, calls=%fused_computation.129 | convolution fusion | flops 5368709120 | bytes 47710208 | tf_op jit(solution)/shard_map/dot_general | solution.py:70
  891.9 4.5 slice.182
  897.8 5.6 copy.56
  906.4 14.2 all-gather.9.cloned.1.call-done
  920.5 3.3 copy.57
  927.0 41.7 %all-gather.11.cloned.1.call-done = bf16[1,1024,2048]{1,2,0:T(8,128)(2,1)} async-done(((bf16[1,128,2048]{1,2,0:T(8,128)(2,1)}), bf16[1,1024,2048]{1,2,0:T(8,128)(2,1)}) %all-gather.11.cloned.1.call-update) | async-done | bytes 4194320 | tf_op jit(solution)/shard_map/all_gather | solution.py:159
  968.6 3.3 copy.58
  975.0 68.7 %while.35 = (s32[]{:T(128)}, f32[1,32,128,64]{2,3,1,0:T(8,128)}, f32[1,32,128]{2,1,0:T(8,128)S(1)}, f32[1,32,128]{2,1,0:T(8,128)S(1)}, s32[8]{0:T(128)S(1)}, /*i...) while((s32[]{:T(128)}, f32[1,32,128,64]{2,3,1,0:T(8,128)}, ...), condition=%wide.region_5.6_spmd.clone, body=%wide.region_2.5_spmd.clone.sunk | while | flops 141861120 | bytes 10291419 | solution.py:175
  1045.3 208.6 %while.36 = (s32[]{:T(128)}, bf16[2,1,128,2048]{2,3,1,0:T(8,128)(2,1)}, f32[2,1,128,2048]{2,3,1,0:T(8,128)}, f32[1,128,32,64]{1,3,2,0:T(8,128)}, s32[]{:T(128)},...) while((s32[]{:T(128)}, ...), condition=%wide.region_8.9_spmd.clone, body=%wide.region_7.8_spmd.clone.sunk | while | flops 343425280 | bytes 50923972 | solution.py:277
  1058.0 10.2 collective-permute-done.1
  1077.2 4.6 collective-permute-start.1
  1081.8 5.4 collective-permute-start
  1102.6 11.4 collective-permute-start.1
  1114.0 5.4 collective-permute-start
  1119.4 3.2 fusion.138
  1131.7 14.4 collective-permute-start.1
  1146.1 5.4 collective-permute-start
  1151.5 3.2 fusion.138
  1163.8 14.4 collective-permute-start.1
  1178.2 5.4 collective-permute-start
  1183.7 3.2 fusion.138
  1196.0 14.4 collective-permute-start.1
  1210.4 5.4 collective-permute-start
  1215.8 3.2 fusion.138
  1228.1 14.4 collective-permute-start.1
  1242.5 5.4 collective-permute-start
  1259.7 14.5 collective-permute-start.2
  1274.2 5.0 convert_reduce_fusion
  1285.4 10.0 broadcast_in_dim.103
  1295.4 3.4 pad_maximum_fusion.2
  1298.8 8.4 collective-permute-start.3
  1312.3 4.5 all-to-all-start.1
  1318.1 3.5 collective-permute-start.4
  1324.8 39.2 %collective-permute-done.3 = bf16[128,14336]{1,0:T(8,128)(2,1)} collective-permute-done((bf16[128,14336]{1,0:T(8,128)(2,1)}, bf16[128,14336]{1,0:T(8,128)(2,1)}, u32[]{:S(2)}, u32[]{:S(2)}) %collective-permute-start.3) | collective-permute-done | bytes 3670048 | tf_op jit(solution)/shard_map/ppermute | solution.py:20
  1364.0 17.3 collective-permute-start.5
  1381.3 27.9 %multiply_reduce_fusion = (f32[2048]{0:T(1024)}, f32[128]{0:T(128)S(1)}, f32[128]{0:T(128)S(1)}, f32[2048]{0:T(1024)}, f32[128,2048]{1,0:T(8,128)}) fusion(bf16[1,128,2048]{2,1,0:T(8,128)(2,1)S(1)} %copy-done.7, f32[128]{0:T(128)S(1)} %add_rsqrt_fusion, f32[128]{0:T(128)S(1)} %broadcast_multiply_fusion.2, f32[2048]{0:T(1024)S(1)} %copy-done.17, ...), kind=kOutput, calls=%fused_computation.107 | convolution fusion | flops 7526150144 | bytes 63989760 | tf_op jit(solution)/shard_map/dot_general | solution.py:70
  1409.2 3.5 convert_reduce_fusion.2
  1412.8 39.2 %all-to-all-start = ((bf16[128,8,256]{2,0,1:T(8,128)(2,1)}), bf16[128,8,256]{2,0,1:T(8,128)(2,1)}, u32[]{:S(2)}, u32[]{:S(2)}) async-start(bf16[128,8,256]{2,0,1:T(8,128)(2,1)} %fusion.55), calls=%async_computation | async-start | bytes 1048576 | tf_op jit(solution)/shard_map/all_to_all | solution.py:205
  1454.5 3.5 collective-permute-start.6
  1458.1 10.0 convolution_convert_fusion.1
  1471.0 17.6 collective-permute-start.7
  1488.7 4.2 constant_dynamic-update-slice_fusion.6
  1492.8 4.2 constant_dynamic-update-slice_fusion.5
  1497.1 45.6 %collective-permute-done.6 = bf16[128,14336]{1,0:T(8,128)(2,1)} collective-permute-done((bf16[128,14336]{1,0:T(8,128)(2,1)}, bf16[128,14336]{1,0:T(8,128)(2,1)}, u32[]{:S(2)}, u32[]{:S(2)}) %collective-permute-start.6) | collective-permute-done | bytes 3670048 | tf_op jit(solution)/shard_map/ppermute | solution.py:23
  1542.7 3.7 collective-permute-start.8
  1546.4 4.2 constant_dynamic-update-slice_fusion.4
  1550.5 5.9 collective-permute-done.7
  1556.4 17.1 collective-permute-start.9
  1573.5 4.2 constant_dynamic-update-slice_fusion.3
  1579.8 45.7 %collective-permute-done.8 = bf16[128,14336]{1,0:T(8,128)(2,1)S(1)} collective-permute-done((bf16[128,14336]{1,0:T(8,128)(2,1)}, bf16[128,14336]{1,0:T(8,128)(2,1)S(1)}, u32[]{:S(2)}, u32[]{:S(2)}) %collective-permute-start.8) | collective-permute-done | bytes 3670048 | tf_op jit(solution)/shard_map/ppermute | solution.py:23
  1627.7 6.2 collective-permute-done.9
  1636.0 15.6 convolution_convert_fusion
  1651.7 66.2 %pmax.7 = f32[32]{0:T(128)S(1)} all-reduce(f32[32]{0:T(128)S(1)} %get-tuple-element.486), channel_id=1, replica_groups=mesh['dp'=4,'ctx'=8] {'dp','ctx'}, use_global_device_ids=true, to_apply=%region_24.25 | all-reduce | flops 32 | bytes 256 | tf_op jit(solution)/shard_map/pmax | solution.py:179
  1718.7 4.1 convert_multiply_fusion
  1722.8 18.6 fusion.46
  1741.4 177.2 %all-reduce.7.cloned.1.call-done = (bf16[256,14336]{1,0:T(8,128)(2,1)}, bf16[1280,2048]{1,0:T(8,128)(2,1)}) async-done(((bf16[256,14336]{1,0:T(8,128)(2,1)}, bf16[1280,2048]{1,0:T(8,128)(2,1)}), (bf16[256,14336]{1,0:T(8,128)(2,1)}, bf16[1280,2048]{1,0:T(8,128)(2,1)})) %all-reduce.7.cloned.1.call-update) | async-done | bytes 12582928 | tf_op jit(solution)/shard_map/psum | solution.py:306
  1918.6 6.0 slice.183
  1924.5 4.4 slice.185
  1930.5 4.4 slice.186
  (375 shorter events, 191.0 us)
Async XLA Ops:
  7.2 505.4 %all-gather.7.cloned.1.call-start = ((), (), s32[]{:S(2)}) async-start(), calls=%async_computation.2 | async-start | bytes 66060288 | tf_op jit(solution)/shard_map/all_gather | solution.py:138
  14.2 857.7 %all-gather.13.cloned.1.call-start = ((), (), s32[]{:S(2)}) async-start(), calls=%async_computation.5 | async-start | bytes 47185920 | tf_op jit(solution)/shard_map/all_gather | solution.py:194
  20.8 491.8 %copy-start.17 = (f32[2048]{0:T(1024)S(1)}, f32[2048]{0:T(1024)}, u32[]{:S(2)}) copy-start(f32[2048]{0:T(1024)} %param.20) | copy-start | bytes 24580
  20.8 491.8 %copy-start.18 = (f32[2048]{0:T(1024)S(1)}, f32[2048]{0:T(1024)}, u32[]{:S(2)}) copy-start(f32[2048]{0:T(1024)} %param.21) | copy-start | bytes 24580
  20.9 899.7 %all-gather.9.cloned.1.call-start = ((), (), s32[]{:S(2)}) async-start(), calls=%async_computation.3 | async-start | bytes 4718592 | tf_op jit(solution)/shard_map/all_gather | solution.py:158
  22.3 520.5 %copy-start.19 = (f32[6144]{0:T(1024)S(1)}, f32[6144]{0:T(1024)}, u32[]{:S(2)}) copy-start(f32[6144]{0:T(1024)} %param.23) | copy-start | bytes 73732
  549.1 322.8 %copy-start.14 = (bf16[1,128,2048]{2,1,0:T(8,128)(2,1)S(1)}, bf16[1,128,2048]{2,1,0:T(8,128)(2,1)}, u32[]{:S(2)}) copy-start(bf16[1,128,2048]{2,1,0:T(8,128)(2,1)} %param.31) | copy-start | bytes 1572868
  551.0 417.7 %all-gather.11.cloned.1.call-start = ((), (), s32[]{:S(2)}) async-start(), calls=%async_computation.4 | async-start | bytes 4718592 | tf_op jit(solution)/shard_map/all_gather | solution.py:159
  553.1 904.9 %all-gather.15.cloned.1.call-start = ((), (), s32[]{:S(2)}) async-start(), calls=%async_computation.6 | async-start | bytes 4718592 | tf_op jit(solution)/shard_map/all_gather | solution.py:208
  903.4 1.9 copy-start.11
  903.4 1.9 copy-start.12
  1049.1 1.6 copy-start
  1051.9 16.3 collective-permute-start.1
  1052.2 18.7 collective-permute-start
  1074.4 1.6 copy-start
  1077.2 16.3 collective-permute-start.1
  1081.8 14.4 collective-permute-start
  1099.8 1.6 copy-start
  1102.6 20.0 %collective-permute-start.1 = (bf16[2,1,128,2048]{2,3,1,0:T(8,128)(2,1)}, bf16[2,1,128,2048]{2,3,1,0:T(8,128)(2,1)}, u32[]{:S(2)}, u32[]{:S(2)}) collective-permute-start(bf16[2,1,128,2048]{2,3,1,0:T(8,128)(2,1)} %fusion.137), channel_id=1, source_target_pairs={{0,1},{1,2},{2,3},{3,4},{4,5},{5,6},{6,7},{7,0},{8,9},{9,10},{10,1... | collective-permute-start | bytes 3145736 | tf_op jit(solution)/shard_map/while/body/eval_jaxpr/ppermute | solution.py:39
  1114.0 11.4 collective-permute-start
  1131.7 23.1 %collective-permute-start.1 = (bf16[2,1,128,2048]{2,3,1,0:T(8,128)(2,1)}, bf16[2,1,128,2048]{2,3,1,0:T(8,128)(2,1)}, u32[]{:S(2)}, u32[]{:S(2)}) collective-permute-start(bf16[2,1,128,2048]{2,3,1,0:T(8,128)(2,1)} %fusion.137), channel_id=1, source_target_pairs={{0,1},{1,2},{2,3},{3,4},{4,5},{5,6},{6,7},{7,0},{8,9},{9,10},{10,1... | collective-permute-start | bytes 3145736 | tf_op jit(solution)/shard_map/while/body/eval_jaxpr/ppermute | solution.py:39
  1146.1 11.4 collective-permute-start
  1161.0 1.6 copy-start
  1163.8 23.1 %collective-permute-start.1 = (bf16[2,1,128,2048]{2,3,1,0:T(8,128)(2,1)}, bf16[2,1,128,2048]{2,3,1,0:T(8,128)(2,1)}, u32[]{:S(2)}, u32[]{:S(2)}) collective-permute-start(bf16[2,1,128,2048]{2,3,1,0:T(8,128)(2,1)} %fusion.137), channel_id=1, source_target_pairs={{0,1},{1,2},{2,3},{3,4},{4,5},{5,6},{6,7},{7,0},{8,9},{9,10},{10,1... | collective-permute-start | bytes 3145736 | tf_op jit(solution)/shard_map/while/body/eval_jaxpr/ppermute | solution.py:39
  1178.2 11.4 collective-permute-start
  1196.0 23.1 %collective-permute-start.1 = (bf16[2,1,128,2048]{2,3,1,0:T(8,128)(2,1)}, bf16[2,1,128,2048]{2,3,1,0:T(8,128)(2,1)}, u32[]{:S(2)}, u32[]{:S(2)}) collective-permute-start(bf16[2,1,128,2048]{2,3,1,0:T(8,128)(2,1)} %fusion.137), channel_id=1, source_target_pairs={{0,1},{1,2},{2,3},{3,4},{4,5},{5,6},{6,7},{7,0},{8,9},{9,10},{10,1... | collective-permute-start | bytes 3145736 | tf_op jit(solution)/shard_map/while/body/eval_jaxpr/ppermute | solution.py:39
  1210.4 11.4 collective-permute-start
  1228.1 23.1 %collective-permute-start.1 = (bf16[2,1,128,2048]{2,3,1,0:T(8,128)(2,1)}, bf16[2,1,128,2048]{2,3,1,0:T(8,128)(2,1)}, u32[]{:S(2)}, u32[]{:S(2)}) collective-permute-start(bf16[2,1,128,2048]{2,3,1,0:T(8,128)(2,1)} %fusion.137), channel_id=1, source_target_pairs={{0,1},{1,2},{2,3},{3,4},{4,5},{5,6},{6,7},{7,0},{8,9},{9,10},{10,1... | collective-permute-start | bytes 3145736 | tf_op jit(solution)/shard_map/while/body/eval_jaxpr/ppermute | solution.py:39
  1242.5 11.4 collective-permute-start
  1257.2 17.0 slice-start
  1257.6 1.8 copy-start.1
  1257.6 16.6 slice-start.1
  1258.7 15.5 copy-start.8
  1258.7 15.5 copy-start.21
  1259.7 19.6 %copy-start.4 = (f32[1,128,32,64]{1,3,2,0:T(8,128)S(1)}, f32[1,128,32,64]{1,3,2,0:T(8,128)}, u32[]{:S(2)}) copy-start(f32[1,128,32,64]{1,3,2,0:T(8,128)} %get-tuple-element.312) | copy-start | bytes 3145732
  1259.7 20.4 %collective-permute-start.2 = (bf16[2,1,128,2048]{2,3,1,0:T(8,128)(2,1)S(1)}, bf16[2,1,128,2048]{2,3,1,0:T(8,128)(2,1)S(1)}, u32[]{:S(2)}, u32[]{:S(2)}) collective-permute-start(bf16[2,1,128,2048]{2,3,1,0:T(8,128)(2,1)S(1)} %fusion.47), channel_id=1, source_target_pairs={{0,1},{1,2},{2,3},{3,4},{4,5},{5,6},{6,7},{7,0},{8,9},{9,10},{10,1... | collective-permute-start | bytes 3145736 | tf_op jit(solution)/shard_map/ppermute | solution.py:39
  1279.3 16.1 copy-start.9
  1285.4 10.0 copy-start.10
  1298.8 11.6 copy-start.13
  1298.8 65.2 %collective-permute-start.3 = (bf16[128,14336]{1,0:T(8,128)(2,1)}, bf16[128,14336]{1,0:T(8,128)(2,1)}, u32[]{:S(2)}, u32[]{:S(2)}) collective-permute-start(bf16[128,14336]{1,0:T(8,128)(2,1)} %get-tuple-element.464), channel_id=1, source_target_pairs={{0,1},{1,2},{2,3},{3,4},{4,5},{5,6},{6,7},{7,0},{8,9},{9,10},{10,1... | collective-permute-start | bytes 11010056 | tf_op jit(solution)/shard_map/ppermute | solution.py:20
  1312.3 4.7 copy-start.7
  1312.3 100.5 %all-to-all-start.1 = ((bf16[128,8,1280]{0,2,1:T(8,128)(2,1)}), bf16[128,8,1280]{0,2,1:T(8,128)(2,1)S(1)}, u32[]{:S(2)}, u32[]{:S(2)}) async-start(bf16[128,8,1280]{0,2,1:T(8,128)(2,1)} %pad_maximum_fusion.3), calls=%async_computation.1 | async-start | bytes 5242880 | tf_op jit(solution)/shard_map/all_to_all | solution.py:204
  1316.8 424.5 %all-reduce.5.cloned.1.call-start = ((), (), s32[]{:S(2)}) async-start(), calls=%async_computation.7 | async-start | bytes 163840 | tf_op jit(solution)/shard_map/psum | solution.py:308
  1318.1 136.4 %collective-permute-start.4 = (bf16[128,14336]{1,0:T(8,128)(2,1)}, bf16[128,14336]{1,0:T(8,128)(2,1)}, u32[]{:S(2)}, u32[]{:S(2)}) collective-permute-start(bf16[128,14336]{1,0:T(8,128)(2,1)} %get-tuple-element.464), channel_id=1, source_target_pairs={{0,7},{1,0},{2,1},{3,2},{4,3},{5,4},{6,5},{7,6},{8,15},{9,8},{10,9... | collective-permute-start | bytes 11010056 | tf_op jit(solution)/shard_map/ppermute | solution.py:23
  1364.0 107.0 %collective-permute-start.5 = (bf16[128,14336]{1,0:T(8,128)(2,1)}, bf16[128,14336]{1,0:T(8,128)(2,1)}, u32[]{:S(2)}, u32[]{:S(2)}) collective-permute-start(bf16[128,14336]{1,0:T(8,128)(2,1)} %collective-permute-done.3), channel_id=1, source_target_pairs={{0,1},{1,2},{2,3},{3,4},{4,5},{5,6},{6,7},{7,0},{8,9},{9,10},{10,1... | collective-permute-start | bytes 11010056 | tf_op jit(solution)/shard_map/ppermute | solution.py:20
  1412.8 223.2 %all-to-all-start = ((bf16[128,8,256]{2,0,1:T(8,128)(2,1)}), bf16[128,8,256]{2,0,1:T(8,128)(2,1)}, u32[]{:S(2)}, u32[]{:S(2)}) async-start(bf16[128,8,256]{2,0,1:T(8,128)(2,1)} %fusion.55), calls=%async_computation | async-start | bytes 1048576 | tf_op jit(solution)/shard_map/all_to_all | solution.py:205
  1451.9 466.6 %all-reduce.7.cloned.1.call-start = ((), (), s32[]{:S(2)}) async-start(), calls=%async_computation.8 | async-start | bytes 25165824 | tf_op jit(solution)/shard_map/psum | solution.py:306
  1454.5 88.1 %collective-permute-start.6 = (bf16[128,14336]{1,0:T(8,128)(2,1)}, bf16[128,14336]{1,0:T(8,128)(2,1)}, u32[]{:S(2)}, u32[]{:S(2)}) collective-permute-start(bf16[128,14336]{1,0:T(8,128)(2,1)} %collective-permute-done.4), channel_id=1, source_target_pairs={{0,7},{1,0},{2,1},{3,2},{4,3},{5,4},{6,5},{7,6},{8,15},{9,8},{10,9... | collective-permute-start | bytes 11010056 | tf_op jit(solution)/shard_map/ppermute | solution.py:23
  1471.0 85.4 %collective-permute-start.7 = (bf16[128,14336]{1,0:T(8,128)(2,1)}, bf16[128,14336]{1,0:T(8,128)(2,1)S(1)}, u32[]{:S(2)}, u32[]{:S(2)}) collective-permute-start(bf16[128,14336]{1,0:T(8,128)(2,1)} %collective-permute-done.5), channel_id=1, source_target_pairs={{0,1},{1,2},{2,3},{3,4},{4,5},{5,6},{6,7},{7,0},{8,9},{9,10},{10,1... | collective-permute-start | bytes 11010056 | tf_op jit(solution)/shard_map/ppermute | solution.py:20
  1542.7 82.8 %collective-permute-start.8 = (bf16[128,14336]{1,0:T(8,128)(2,1)}, bf16[128,14336]{1,0:T(8,128)(2,1)S(1)}, u32[]{:S(2)}, u32[]{:S(2)}) collective-permute-start(bf16[128,14336]{1,0:T(8,128)(2,1)} %collective-permute-done.6), channel_id=1, source_target_pairs={{0,7},{1,0},{2,1},{3,2},{4,3},{5,4},{6,5},{7,6},{8,15},{9,8},{10,9... | collective-permute-start | bytes 11010056 | tf_op jit(solution)/shard_map/ppermute | solution.py:23
  1556.4 77.4 %collective-permute-start.9 = (bf16[128,14336]{1,0:T(8,128)(2,1)S(1)}, bf16[128,14336]{1,0:T(8,128)(2,1)S(1)}, u32[]{:S(2)}, u32[]{:S(2)}) collective-permute-start(bf16[128,14336]{1,0:T(8,128)(2,1)S(1)} %collective-permute-done.7), channel_id=1, source_target_pairs={{0,1},{1,2},{2,3},{3,4},{4,5},{5,6},{6,7},{7,0},{8,9},{9,10},{10,1... | collective-permute-start | bytes 11010056 | tf_op jit(solution)/shard_map/ppermute | solution.py:20
  1651.6 66.2 %copy-start.30 = (s32[32]{0:T(128)S(1)}, s32[32]{0:T(128)}, u32[]{:S(2)}) copy-start(s32[32]{0:T(128)} %param.30) | copy-start | bytes 388
  1651.6 66.4 %copy-start.20 = (f32[6144]{0:T(1024)S(1)}, f32[6144]{0:T(1024)}, u32[]{:S(2)}) copy-start(f32[6144]{0:T(1024)} %param.23) | copy-start | bytes 73732
  1651.6 71.1 %copy-start.27 = (f32[2048]{0:T(1024)S(1)}, f32[2048]{0:T(1024)}, u32[]{:S(2)}) copy-start(f32[2048]{0:T(1024)} %param.29) | copy-start | bytes 24580
  1651.7 71.1 %copy-start.28 = (f32[2048]{0:T(1024)S(1)}, f32[2048]{0:T(1024)}, u32[]{:S(2)}) copy-start(f32[2048]{0:T(1024)} %param.25) | copy-start | bytes 24580
  1717.9 23.5 %copy-start.31 = (f32[32]{0:T(128)}, f32[32]{0:T(128)S(1)}, u32[]{:S(2)}) copy-start(f32[32]{0:T(128)S(1)} %pmax.7) | copy-start | bytes 388
  1918.5 6.0 copy-start.5
  1918.5 10.4 slice-start.2
  1924.5 4.4 slice-start.3
  1930.5 4.5 copy-start.23
  1930.5 5.1 copy-start.26
  1930.5 5.7 copy-start.25
  1930.5 6.3 copy-start.24
  1930.5 7.5 copy-start.22
  (21 other events, 29.3 us)
Sparse Core Ops, SparseCore 0:
  14.4 498.2 all-gather.6
  514.8 357.0 all-gather.12
  874.1 46.3 all-gather.8
  922.5 46.0 all-gather.10
  970.1 45.3 all-gather.14
  1412.9 165.9 all-reduce.4
  1651.8 266.7 all-reduce.6
